TPU v7x, 256 devices: a whole 4x4x8 slice. The times are simulated.
256 devices in a mesh: seq: 32 (over z, x_hi, core), tp: 8 (over x_lo, y).
Axes of the slice: x: 4 (x_hi: 2, x_lo: 2; x = x_hi * 2 + x_lo), y: 4, z: 8, core: 2. Of those that a mesh axis runs over, the one named last changes fastest.
Arguments:
- query: bfloat16 [8192, 3584], P('seq', 'tp'), may hold values from -6 to 6
- keys: bfloat16 [8192, 3584], P('seq', 'tp'), may hold values from -6 to 6
- values: bfloat16 [8192, 3584], P('seq', 'tp'), may hold values from -6 to 6
- prefix_keys: bfloat16 [4096, 3584], P('seq', 'tp'), may hold values from -6 to 6
- prefix_values: bfloat16 [4096, 3584], P('seq', 'tp'), may hold values from -6 to 6
- residual: bfloat16 [8192, 3584], P('seq', 'tp'), may hold values from -4 to 4
- out_weight: bfloat16 [3584, 3584], P('tp'), may hold values from -1 to 1
- suffix_lens: int32 [16], replicated, may hold values from 1 to 2048, 8192 in all
- req_group: int32 [16], replicated, may hold values from 0 to 3
- placement: int32 [8192], replicated, may hold values from 0 to 8191, each once
- prefix_owner: int32 [32], replicated, may hold values from 0 to 3, as said below
Outputs:
- hidden: bfloat16 [8192, 3584], P('seq', 'tp')
- cache_keys: bfloat16 [8192, 3584], P('seq', 'tp')
- cache_values: bfloat16 [8192, 3584], P('seq', 'tp')
Inputs may be any that keep to these rules, and one draw needn't show every extreme that they name: `prefix_owner`: each group number appears exactly 8 times.
All inputs are finite; a program needn't handle non-finite values.
Results may differ from a plain program's by a relative error of at most 0.014.
Values may be sent and summed in bfloat16 or wider, within the bound.
A program may use at most 128 MiB of HBM per device.

v0:
```python
import math
import jax
import jax.numpy as jnp
from jax import lax
from jax.sharding import PartitionSpec as P

HD = 224
NEG_FILL = -1e30


def request_of(positions, ends):
    return jnp.sum((positions[:, None] >= ends[None, :]).astype(jnp.int32), axis=1)


def lookup_small(indices, table):
    slots = jnp.arange(table.shape[0], dtype=jnp.int32)
    return jnp.sum(jnp.where(indices[:, None] == slots[None, :], table[None, :], 0), axis=1)


def absorb(state, query_heads, key_piece, value_piece, visible):
    top, total, accum = state
    count = key_piece.shape[0]
    heads = query_heads.shape[1]
    head_size = query_heads.shape[2]
    key_heads = key_piece.reshape(count, heads, head_size)
    value_heads = value_piece.reshape(count, heads, head_size)
    scores = jnp.einsum(
        "qhd,khd->hqk", query_heads, key_heads, preferred_element_type=jnp.float32
    ) * (1.0 / math.sqrt(head_size))
    scores = jnp.where(visible[None], scores, NEG_FILL)
    fresh = jnp.maximum(top, jnp.max(scores, axis=2))
    weights = jnp.where(visible[None], jnp.exp(scores - fresh[:, :, None]), 0.0).astype(
        jnp.bfloat16
    )
    factor = jnp.exp(top - fresh)
    total = factor * total + jnp.sum(weights.astype(jnp.float32), axis=2)
    accum = factor[:, :, None] * accum + jnp.einsum(
        "hqk,khd->hqd", weights, value_heads, preferred_element_type=jnp.float32
    )
    return (fresh, total, accum)


def shards(
    query,
    keys,
    values,
    prefix_keys,
    prefix_values,
    residual,
    out_weight,
    suffix_lens,
    req_group,
    placement,
    prefix_owner,
):
    rows, width = query.shape
    block_rows = prefix_keys.shape[0]
    heads = width // HD
    me = lax.axis_index("seq")
    ends = jnp.cumsum(suffix_lens)
    my_pos = lax.dynamic_slice_in_dim(placement, me * rows, rows)
    my_req = request_of(my_pos, ends)
    my_grp = lookup_small(my_req, req_group)
    query_heads = query.reshape(rows, heads, HD)
    start_state = (
        jnp.full((heads, rows), NEG_FILL, jnp.float32),
        jnp.zeros((heads, rows), jnp.float32),
        jnp.zeros((heads, rows, HD), jnp.float32),
    )
    empty_cache = jnp.zeros((rows, width), jnp.bfloat16)
    pieces = (
        lax.all_gather(keys, "seq", axis=0, tiled=True),
        lax.all_gather(values, "seq", axis=0, tiled=True),
    )
    state = start_state
    cache = (empty_cache, empty_cache)
    count = pieces[0].shape[0]
    valid = jnp.ones((count,), jnp.bool_)
    key_req = request_of(placement, ends)
    state = absorb(
        state,
        query_heads,
        pieces[0],
        pieces[1],
        valid[None, :]
        & (key_req[None, :] == my_req[:, None])
        & (placement[None, :] <= my_pos[:, None]),
    )
    local = placement - me * rows
    keep = valid & (local >= 0) & (local < rows)
    target = jnp.where(keep, local, rows)
    cache = (
        cache[0].at[target].set(pieces[0], mode="drop"),
        cache[1].at[target].set(pieces[1], mode="drop"),
    )
    state, cache = (state, cache)
    pieces = (
        lax.all_gather(prefix_keys, "seq", axis=0, tiled=True),
        lax.all_gather(prefix_values, "seq", axis=0, tiled=True),
    )
    count = pieces[0].shape[0]
    key_block = jnp.arange(count, dtype=jnp.int32) // block_rows
    valid = jnp.ones((count,), jnp.bool_)
    key_grp = lookup_small(key_block, prefix_owner)
    state = absorb(
        state,
        query_heads,
        pieces[0],
        pieces[1],
        valid[None, :] & (key_grp[None, :] == my_grp[:, None]),
    )
    top, total, accum = state
    attended = accum / total[:, :, None]
    attended = jnp.transpose(attended, (1, 0, 2)).reshape(rows, width).astype(jnp.bfloat16)
    term = jnp.dot(attended, out_weight, preferred_element_type=jnp.float32)
    summed = lax.psum_scatter(
        term.astype(jnp.bfloat16), "tp", scatter_dimension=1, tiled=True
    ).astype(jnp.float32)
    hidden = (residual.astype(jnp.float32) + summed).astype(jnp.bfloat16)
    return (hidden, cache[0], cache[1])


def solution(mesh):
    return jax.shard_map(
        shards,
        mesh=mesh,
        in_specs=(
            P("seq", "tp"),
            P("seq", "tp"),
            P("seq", "tp"),
            P("seq", "tp"),
            P("seq", "tp"),
            P("seq", "tp"),
            P("tp", None),
            P(),
            P(),
            P(),
            P(),
        ),
        out_specs=(P("seq", "tp"), P("seq", "tp"), P("seq", "tp")),
        check_vma=False,
    )
```

profile of v0, /device:TPU:1, one launch (start us, length us, event | category | flops | bytes accessed | tf_op | source)
XLA Modules:
  0.0 508.1 jit_solution(1577933013104015989)
XLA Ops:
  7.2 0.7 all-gather.7.cloned.1.call-update
  8.0 0.7 all-gather.5.cloned.1.call-update
  8.7 0.7 all-gather.11.cloned.1.call-update
  9.4 0.5 all-gather.9.cloned.1.call-update
  10.0 0.0 reduce-scatter.2.cloned.1.call-start
  10.0 0.7 copy.20
  10.8 0.1 reduce
  10.9 0.8 dynamic_slice.3
  11.7 0.1 convert_reduce_fusion.3
  11.8 0.7 select_reduce_fusion.1
  12.5 0.9 convert_reduce_fusion.2
  13.4 0.8 select_reduce_fusion
  14.3 1.6 broadcast_compare_fusion
  15.9 3.6 compare_and_fusion
  19.4 79.9 %all-gather.7.cloned.1.call-done = bf16[4096,448]{0,1:T(8,128)(2,1)} async-done(((bf16[128,448]{0,1:T(8,128)(2,1)}), bf16[4096,448]{0,1:T(8,128)(2,1)}) %all-gather.7.cloned.1.call-update) | async-done | bytes 3670032 | tf_op jit(solution)/shard_map/all_gather | solution.py:98
  99.3 7.9 %fusion.1 = (f32[2,256]{1,0:T(2,128)S(1)}, f32[2,256,4096]{2,1,0:T(8,128)}) fusion(pred[256,4096]{1,0:T(8,128)(4,1)} %broadcast_compare_fusion, bf16[256,2,224]{0,2,1:T(8,128)(2,1)} %bitcast.56, bf16[4096,2,224]{0,2,1:T(8,128)(2,1)} %bitcast.55), kind=kOutput, calls=%fused_computation.10 | convolution fusion | flops 945815040 | bytes 13338624 | tf_op jit(solution)/shard_map/qhd,khd->hqk/dot_general | solution.py:27
  107.2 94.4 %all-gather.5.cloned.1.call-done = bf16[8192,448]{0,1:T(8,128)(2,1)} async-done(((bf16[256,448]{0,1:T(8,128)(2,1)}), bf16[8192,448]{0,1:T(8,128)(2,1)}) %all-gather.5.cloned.1.call-update) | async-done | bytes 7340048 | tf_op jit(solution)/shard_map/all_gather | solution.py:72
  201.6 12.2 %fusion = (f32[2,256]{1,0:T(2,128)S(1)}, f32[2,256,8192]{2,1,0:T(8,128)}) fusion(pred[256,8192]{1,0:T(8,128)(4,1)} %compare_and_fusion, bf16[256,2,224]{0,2,1:T(8,128)(2,1)S(1)} %bitcast.57, bf16[8192,2,224]{0,2,1:T(8,128)(2,1)} %bitcast.50), kind=kOutput, calls=%fused_computation.5 | convolution fusion | flops 1891630592 | bytes 26445824 | tf_op jit(solution)/shard_map/qhd,khd->hqk/dot_general | solution.py:27
  213.9 2.7 convert_reduce_fusion.1
  216.5 8.6 %convert_reduce_fusion = f32[2,256]{1,0:T(2,128)S(1)} fusion(f32[2,256]{1,0:T(2,128)S(1)} %get-tuple-element.12, f32[2,256,8192]{2,1,0:T(8,128)} %get-tuple-element.15, pred[256,8192]{1,0:T(8,128)(4,1)S(1)} %copy-done.1), kind=kLoop, calls=%fused_computation.2 | loop fusion | flops 29359616 | bytes 18878464 | tf_op jit(solution)/shard_map/reduce_sum | solution.py:36
  225.1 59.9 %all-gather.11.cloned.1.call-done = bf16[4096,448]{0,1:T(8,128)(2,1)} async-done(((bf16[128,448]{0,1:T(8,128)(2,1)}), bf16[4096,448]{0,1:T(8,128)(2,1)}) %all-gather.11.cloned.1.call-update) | async-done | bytes 3670032 | tf_op jit(solution)/shard_map/all_gather | solution.py:99
  285.0 7.7 %convolution_bitcast_fusion = f32[256,2,224]{0,2,1:T(8,128)} fusion(bf16[4096,2,224]{0,2,1:T(8,128)(2,1)} %bitcast.54, f32[2,256,4096]{2,1,0:T(8,128)} %get-tuple-element.17, f32[2,256]{1,0:T(2,128)S(1)} %get-tuple-element.13, pred[256,4096]{1,0:T(8,128)(4,1)} %broadcast_compare_fusion), kind=kOutput, calls=%fused_computation.13 | convolution fusion | flops 950009856 | bytes 13568000 | tf_op jit(solution)/shard_map/hqk,khd->hqd/dot_general | solution.py:37
  292.8 94.4 %all-gather.9.cloned.1.call-done = bf16[8192,448]{0,1:T(8,128)(2,1)} async-done(((bf16[256,448]{0,1:T(8,128)(2,1)}), bf16[8192,448]{0,1:T(8,128)(2,1)}) %all-gather.9.cloned.1.call-update) | async-done | bytes 7340048 | tf_op jit(solution)/shard_map/all_gather | solution.py:73
  387.2 13.2 %fusion.6 = bf16[256,2,224]{0,2,1:T(8,128)(2,1)S(1)} fusion(f32[256,2,224]{0,2,1:T(8,128)} %convolution_bitcast_fusion, bf16[8192,2,224]{0,2,1:T(8,128)(2,1)} %bitcast.51, f32[256,2]{0,1:T(2,128)S(1)} %get-tuple-element.9, f32[256,2]{0,1:T(2,128)S(1)} %get-tuple-element.11, f32[256,2]{0,1:T(2,128)S(1)} %get-tuple-element.10, ...), kind=kOutput, calls=%fused_computation.19 | convolution fusion | flops 1900593152 | bytes 26910720 | tf_op jit(solution)/shard_map/hqk,khd->hqd/dot_general | solution.py:37
  400.4 2.9 convolution_convert_fusion
  403.3 11.6 %copy.21 = bf16[8192,448]{1,0:T(8,128)(2,1)} copy(bf16[8192,448]{0,1:T(8,128)(2,1)} %all-gather.5.cloned.1.call-done) | data formatting | bytes 14680064 | tf_op jit(solution)/shard_map/all_gather | solution.py:72
  414.9 35.8 %scatter_custom_fusion = bf16[256,448]{1,0:T(8,128)(2,1)S(1)} fusion(s32[8192]{0:T(1024)S(1)} %compare_select_fusion, bf16[8192,448]{1,0:T(8,128)(2,1)} %copy.21, bf16[]{:T(256)} %constant.47.clone.1), kind=kCustom, calls=%fused_computation.26 | custom fusion | bytes 229888 | tf_op jit(solution)/shard_map/scatter | solution.py:93
  450.7 0.8 copy.23
  451.5 11.6 %copy.22 = bf16[8192,448]{1,0:T(8,128)(2,1)} copy(bf16[8192,448]{0,1:T(8,128)(2,1)} %all-gather.9.cloned.1.call-done) | data formatting | bytes 14680064 | tf_op jit(solution)/shard_map/all_gather | solution.py:73
  463.1 35.8 %scatter_custom_fusion.1 = bf16[256,448]{1,0:T(8,128)(2,1)S(1)} fusion(s32[8192]{0:T(1024)S(1)} %compare_select_fusion, bf16[8192,448]{1,0:T(8,128)(2,1)} %copy.22, bf16[]{:T(256)} %constant.47.clone.1), kind=kCustom, calls=%fused_computation.24 | custom fusion | bytes 229888 | tf_op jit(solution)/shard_map/scatter | solution.py:94
  498.9 0.8 copy.24
  499.8 1.8 add_convert_fusion
  (23 shorter events, 0.3 us)
Async XLA Ops:
  7.2 393.2 %copy-start = (bf16[448,3584]{1,0:T(8,128)(2,1)S(1)}, bf16[448,3584]{1,0:T(8,128)(2,1)}, u32[]{:S(2)}) copy-start(bf16[448,3584]{1,0:T(8,128)(2,1)} %param.17) | copy-start | bytes 9633796
  7.2 92.1 %all-gather.7.cloned.1.call-start = ((), (), s32[]{:S(2)}) async-start(), calls=%async_computation.2 | async-start | bytes 3784704 | tf_op jit(solution)/shard_map/all_gather | solution.py:98
  7.9 193.7 %all-gather.5.cloned.1.call-start = ((), (), s32[]{:S(2)}) async-start(), calls=%async_computation.1 | async-start | bytes 7569408 | tf_op jit(solution)/shard_map/all_gather | solution.py:72
  8.7 276.4 %all-gather.11.cloned.1.call-start = ((), (), s32[]{:S(2)}) async-start(), calls=%async_computation.4 | async-start | bytes 3784704 | tf_op jit(solution)/shard_map/all_gather | solution.py:99
  9.4 377.8 %all-gather.9.cloned.1.call-start = ((), (), s32[]{:S(2)}) async-start(), calls=%async_computation.3 | async-start | bytes 7569408 | tf_op jit(solution)/shard_map/all_gather | solution.py:73
  10.0 489.8 %reduce-scatter.2.cloned.1.call-start = ((), (), s32[]{:S(2)}) async-start(), calls=%async_computation.5 | async-start | bytes 2064384 | tf_op jit(solution)/shard_map/reduce_scatter | solution.py:116
  19.4 182.1 %copy-start.5 = (bf16[256,448]{0,1:T(8,128)(2,1)S(1)}, bf16[256,448]{0,1:T(8,128)(2,1)}, u32[]{:S(2)}) copy-start(bf16[256,448]{0,1:T(8,128)(2,1)} %param.11) | copy-start | bytes 688132
  201.6 12.3 %copy-start.2 = (f32[2,256,4096]{2,1,0:T(8,128)S(1)}, f32[2,256,4096]{2,1,0:T(8,128)}, u32[]{:S(2)}) copy-start(f32[2,256,4096]{2,1,0:T(8,128)} %get-tuple-element.17) | copy-start | bytes 25165828
  201.6 12.3 %copy-start.3 = (pred[256,4096]{1,0:T(8,128)(4,1)S(1)}, pred[256,4096]{1,0:T(8,128)(4,1)}, u32[]{:S(2)}) copy-start(pred[256,4096]{1,0:T(8,128)(4,1)} %broadcast_compare_fusion) | copy-start | bytes 3145732
  213.8 2.7 copy-start.1
  387.2 16.1 %copy-start.4 = (s32[8192]{0:T(1024)S(1)}, s32[8192]{0:T(1024)}, u32[]{:S(2)}) copy-start(s32[8192]{0:T(1024)} %param.20) | copy-start | bytes 98308
Sparse Core Ops, SparseCore 0:
  10.6 88.6 all-gather.6
  101.8 99.6 all-gather.4
  204.1 80.8 all-gather.10
  287.5 99.6 all-gather.8
  403.4 35.0 reduce-scatter.1
where the time goes:
time: 509 us; the launch traced here: 508 us
  waiting for transfers between devices  331 us (65%)
  local copies, waits for them, and re-layouts  98 us (19%)
  matrix products  43.9 us (9%)
  other arithmetic  21 us (4%)
  between operations  13.9 us (3%)
    all_gather x1, waiting for transfers between devices, shards(): lax.all_gather(values, 'seq', axis=0, tiled=True)  94.4 us
    all_gather x1, waiting for transfers between devices, shards(): lax.all_gather(keys, 'seq', axis=0, tiled=True)  94.4 us
    all_gather x1, waiting for transfers between devices, shards(): lax.all_gather(prefix_keys, 'seq', axis=0, tiled=True)  79.9 us
    all_gather x1, waiting for transfers between devices, shards(): lax.all_gather(prefix_values, 'seq', axis=0, tiled=True)  59.9 us
    scatter x1, local copies, waits for them, and re-layouts, shards(): cache[0].at[target].set(pieces[0], mode='drop')  35.8 us
    scatter x1, local copies, waits for them, and re-layouts, shards(): cache[1].at[target].set(pieces[1], mode='drop')  35.8 us
    dot_general x2, matrix products, absorb(): jnp.einsum('hqk,khd->hqd', weights, value_heads, preferred_element_type=j...  20.9 us
    dot_general x2, matrix products, absorb(): jnp.einsum('qhd,khd->hqk', query_heads, key_heads, preferred_element_type...  20.1 us
  transfers between devices with their start and end apart: 5, of which 4 were waited for; matrix products, arithmetic and copies ran while one was open for 29% of the time, Pallas kernels for 0%

commit v1 on v0

--- a/solution.py
+++ b/solution.py
@@ -95,7 +95,9 @@
     )
     state, cache = (state, cache)
     pieces = (
-        lax.all_gather(prefix_keys, "seq", axis=0, tiled=True),
+        jnp.concatenate(
+            lax.all_to_all(jnp.stack([prefix_keys] * lax.axis_size("seq")), "seq", 0, 0), axis=0
+        ),
         lax.all_gather(prefix_values, "seq", axis=0, tiled=True),
     )
     count = pieces[0].shape[0]

time: 509 us -> 467 us (0.917)
  waiting for transfers between devices: 331 us -> 264 us
  local copies, waits for them, and re-layouts: 98 us -> 113 us
  starting transfers between devices: 0.19 us -> 12.8 us
    all_to_all x0 -> x1, waiting for transfers between devices: none -> 90.2 us  [shards(): lax.all_to_all(jnp.stack([prefix_keys] * lax.axis_size('seq')), 'seq', 0, 0)]
    all_gather x1 -> x0, waiting for transfers between devices: 79.9 us -> none  [shards(): lax.all_gather(prefix_keys, 'seq', axis=0, tiled=True)]
    all_gather x1, waiting for transfers between devices: 94.4 us -> 18 us  [shards(): lax.all_gather(keys, 'seq', axis=0, tiled=True)]
    all_to_all x0 -> x1, starting transfers between devices: none -> 12.6 us  [shards(): lax.all_to_all(jnp.stack([prefix_keys] * lax.axis_size('seq')), 'seq', 0, 0)]
    another operation x1 -> x3, local copies, waits for them, and re-layouts: 0.73 us -> 10.3 us  [the longest x1 6.68 us: absorb(): key_heads = key_piece.reshape(count, heads, head_size)]
    all_to_all x0 -> x1, local copies, waits for them, and re-layouts: none -> 6.24 us  [shards(): lax.all_to_all(jnp.stack([prefix_keys] * lax.axis_size('seq')), 'seq', 0, 0)]
  transfers between devices with their start and end apart: 5 -> 5, of which waited for: 4 -> 4; matrix products, arithmetic and copies ran while one was open for 29% -> 34% of each run, Pallas kernels for 0% -> 0%
where the time goes in v1:
time: 467 us; the launch traced here: 466 us
  waiting for transfers between devices  264 us (57%)
  local copies, waits for them, and re-layouts  113 us (24%)
  matrix products  43.9 us (9%)
  other arithmetic  18.4 us (4%)
  between operations  13.9 us (3%)
  starting transfers between devices  12.8 us (3%)
    all_gather x1, waiting for transfers between devices, shards(): lax.all_gather(values, 'seq', axis=0, tiled=True)  94.6 us
    all_to_all x1, waiting for transfers between devices, shards(): lax.all_to_all(jnp.stack([prefix_keys] * lax.axis_size('seq')), 'seq', 0, 0)  90.2 us
    all_gather x1, waiting for transfers between devices, shards(): lax.all_gather(prefix_values, 'seq', axis=0, tiled=True)  58.9 us
    scatter x1, local copies, waits for them, and re-layouts, shards(): cache[0].at[target].set(pieces[0], mode='drop')  35.8 us
    scatter x1, local copies, waits for them, and re-layouts, shards(): cache[1].at[target].set(pieces[1], mode='drop')  35.8 us
    dot_general x2, matrix products, absorb(): jnp.einsum('hqk,khd->hqd', weights, value_heads, preferred_element_type=j...  20.9 us
    dot_general x2, matrix products, absorb(): jnp.einsum('qhd,khd->hqk', query_heads, key_heads, preferred_element_type...  20.2 us
    all_gather x1, waiting for transfers between devices, shards(): lax.all_gather(keys, 'seq', axis=0, tiled=True)  18 us
  transfers between devices with their start and end apart: 5, of which 4 were waited for; matrix products, arithmetic and copies ran while one was open for 34% of the time, Pallas kernels for 0%

profile of v1, /device:TPU:1, one launch (start us, length us, event | category | flops | bytes accessed | tf_op | source)
XLA Modules:
  0.0 465.9 jit_solution(42279962767189021)
XLA Ops:
  7.3 0.7 all-gather.4.cloned.1.call-update
  8.0 0.7 all-gather.8.cloned.1.call-update
  8.8 0.7 all-gather.6.cloned.1.call-update
  9.4 3.6 stack.2
  13.0 12.6 %all-to-all-start = ((bf16[32,128,448]{1,2,0:T(8,128)(2,1)}), bf16[32,128,448]{1,2,0:T(8,128)(2,1)}, u32[]{:S(2)}, u32[]{:S(2)}) async-start(bf16[32,128,448]{1,2,0:T(8,128)(2,1)} %stack.2), calls=%async_computation | async-start | bytes 7340032 | tf_op jit(solution)/shard_map/all_to_all | solution.py:99
  25.8 0.1 reduce
  26.0 0.1 convert_reduce_fusion.3
  26.1 0.1 select_reduce_fusion.1
  26.2 0.2 convert_reduce_fusion.2
  26.4 0.2 select_reduce_fusion
  26.6 1.6 broadcast_compare_fusion
  28.2 2.8 compare_and_fusion
  31.0 90.2 %all-to-all-done = bf16[32,128,448]{1,2,0:T(8,128)(2,1)} async-done(((bf16[32,128,448]{1,2,0:T(8,128)(2,1)}), bf16[32,128,448]{1,2,0:T(8,128)(2,1)}, u32[]{:S(2)}, u32[]{:S(2)}) %all-to-all-start) | async-done | bytes 3670048 | tf_op jit(solution)/shard_map/all_to_all | solution.py:99
  121.2 6.2 %copy.27 = bf16[32,128,448]{1,0,2:T(8,128)(2,1)} copy(bf16[32,128,448]{1,2,0:T(8,128)(2,1)} %all-to-all-done) | data formatting | bytes 7340032 | tf_op jit(solution)/shard_map/all_to_all | solution.py:99
  127.5 6.7 %reshape_reshape.3 = bf16[4096,2,224]{0,2,1:T(8,128)(2,1)} reshape(bf16[32,128,448]{1,0,2:T(8,128)(2,1)} %copy.27) | data formatting | bytes 7340032 | tf_op jit(solution)/shard_map/reshape;reshape | solution.py:25
  134.1 7.9 %fusion.1 = (f32[2,256]{1,0:T(2,128)S(1)}, f32[2,256,4096]{2,1,0:T(8,128)}) fusion(pred[256,4096]{1,0:T(8,128)(4,1)} %broadcast_compare_fusion, bf16[256,2,224]{0,2,1:T(8,128)(2,1)S(1)} %bitcast.56, bf16[4096,2,224]{0,2,1:T(8,128)(2,1)} %reshape_reshape.3), kind=kOutput, calls=%fused_computation.10 | convolution fusion | flops 945815040 | bytes 13338624 | tf_op jit(solution)/shard_map/qhd,khd->hqk/dot_general | solution.py:27
  142.1 18.0 %all-gather.4.cloned.1.call-done = bf16[8192,448]{0,1:T(8,128)(2,1)} async-done(((bf16[256,448]{0,1:T(8,128)(2,1)}), bf16[8192,448]{0,1:T(8,128)(2,1)}) %all-gather.4.cloned.1.call-update) | async-done | bytes 7340048 | tf_op jit(solution)/shard_map/all_gather | solution.py:72
  160.1 12.2 %fusion = (f32[2,256]{1,0:T(2,128)S(1)}, f32[2,256,8192]{2,1,0:T(8,128)}) fusion(pred[256,8192]{1,0:T(8,128)(4,1)} %compare_and_fusion, bf16[256,2,224]{0,2,1:T(8,128)(2,1)S(1)} %bitcast.57, bf16[8192,2,224]{0,2,1:T(8,128)(2,1)} %bitcast.51), kind=kOutput, calls=%fused_computation.5 | convolution fusion | flops 1891630592 | bytes 26445824 | tf_op jit(solution)/shard_map/qhd,khd->hqk/dot_general | solution.py:27
  172.4 2.7 convert_reduce_fusion.1
  175.0 8.8 %convert_reduce_fusion = f32[2,256]{1,0:T(2,128)S(1)} fusion(f32[2,256]{1,0:T(2,128)S(1)} %get-tuple-element.15, f32[2,256,8192]{2,1,0:T(8,128)} %get-tuple-element.18, pred[256,8192]{1,0:T(8,128)(4,1)S(1)} %copy-done.1), kind=kLoop, calls=%fused_computation.2 | loop fusion | flops 29359616 | bytes 18878464 | tf_op jit(solution)/shard_map/reduce_sum | solution.py:36
  183.9 58.9 %all-gather.8.cloned.1.call-done = bf16[4096,448]{0,1:T(8,128)(2,1)} async-done(((bf16[128,448]{0,1:T(8,128)(2,1)}), bf16[4096,448]{0,1:T(8,128)(2,1)}) %all-gather.8.cloned.1.call-update) | async-done | bytes 3670032 | tf_op jit(solution)/shard_map/all_gather | solution.py:101
  242.8 7.7 %convolution_bitcast_fusion = f32[256,2,224]{0,2,1:T(8,128)} fusion(bf16[4096,2,224]{0,2,1:T(8,128)(2,1)} %bitcast.55, f32[2,256,4096]{2,1,0:T(8,128)} %get-tuple-element.20, f32[2,256]{1,0:T(2,128)S(1)} %get-tuple-element.16, pred[256,4096]{1,0:T(8,128)(4,1)} %broadcast_compare_fusion), kind=kOutput, calls=%fused_computation.13 | convolution fusion | flops 950009856 | bytes 13568000 | tf_op jit(solution)/shard_map/hqk,khd->hqd/dot_general | solution.py:37
  250.5 94.6 %all-gather.6.cloned.1.call-done = bf16[8192,448]{0,1:T(8,128)(2,1)} async-done(((bf16[256,448]{0,1:T(8,128)(2,1)}), bf16[8192,448]{0,1:T(8,128)(2,1)}) %all-gather.6.cloned.1.call-update) | async-done | bytes 7340048 | tf_op jit(solution)/shard_map/all_gather | solution.py:73
  345.0 13.2 %fusion.6 = bf16[256,2,224]{0,2,1:T(8,128)(2,1)S(1)} fusion(f32[256,2,224]{0,2,1:T(8,128)} %convolution_bitcast_fusion, bf16[8192,2,224]{0,2,1:T(8,128)(2,1)} %bitcast.52, f32[256,2]{0,1:T(2,128)S(1)} %get-tuple-element.12, f32[256,2]{0,1:T(2,128)S(1)} %get-tuple-element.14, f32[256,2]{0,1:T(2,128)S(1)} %get-tuple-element.13, ...), kind=kOutput, calls=%fused_computation.19 | convolution fusion | flops 1900593152 | bytes 26910720 | tf_op jit(solution)/shard_map/hqk,khd->hqd/dot_general | solution.py:37
  358.2 2.9 convolution_convert_fusion
  361.1 11.6 %copy.28 = bf16[8192,448]{1,0:T(8,128)(2,1)} copy(bf16[8192,448]{0,1:T(8,128)(2,1)} %all-gather.4.cloned.1.call-done) | data formatting | bytes 14680064 | tf_op jit(solution)/shard_map/all_gather | solution.py:72
  372.7 35.8 %scatter_custom_fusion = bf16[256,448]{1,0:T(8,128)(2,1)S(1)} fusion(s32[8192]{0:T(1024)S(1)} %compare_select_fusion, bf16[8192,448]{1,0:T(8,128)(2,1)} %copy.28, bf16[]{:T(256)} %constant.47.clone.1), kind=kCustom, calls=%fused_computation.26 | custom fusion | bytes 229888 | tf_op jit(solution)/shard_map/scatter | solution.py:93
  408.6 0.8 copy.30
  409.4 11.6 %copy.29 = bf16[8192,448]{1,0:T(8,128)(2,1)} copy(bf16[8192,448]{0,1:T(8,128)(2,1)} %all-gather.6.cloned.1.call-done) | data formatting | bytes 14680064 | tf_op jit(solution)/shard_map/all_gather | solution.py:73
  421.0 35.8 %scatter_custom_fusion.1 = bf16[256,448]{1,0:T(8,128)(2,1)S(1)} fusion(s32[8192]{0:T(1024)S(1)} %compare_select_fusion, bf16[8192,448]{1,0:T(8,128)(2,1)} %copy.29, bf16[]{:T(256)} %constant.47.clone.1), kind=kCustom, calls=%fused_computation.24 | custom fusion | bytes 229888 | tf_op jit(solution)/shard_map/scatter | solution.py:94
  456.8 0.8 copy.31
  457.6 1.8 add_convert_fusion
  (31 shorter events, 0.5 us)
Async XLA Ops:
  7.2 351.1 %copy-start = (bf16[448,3584]{1,0:T(8,128)(2,1)S(1)}, bf16[448,3584]{1,0:T(8,128)(2,1)}, u32[]{:S(2)}) copy-start(bf16[448,3584]{1,0:T(8,128)(2,1)} %param.17) | copy-start | bytes 9633796
  7.2 18.5 %copy-start.6 = (s32[16]{0:T(128)S(1)}, s32[16]{0:T(128)}, u32[]{:S(2)}) copy-start(s32[16]{0:T(128)} %param.18) | copy-start | bytes 196
  7.2 18.8 %copy-start.4 = (s32[8192]{0:T(1024)S(1)}, s32[8192]{0:T(1024)}, u32[]{:S(2)}) copy-start(s32[8192]{0:T(1024)} %param.20) | copy-start | bytes 98308
  7.2 18.9 %copy-start.7 = (s32[16]{0:T(128)S(1)}, s32[16]{0:T(128)}, u32[]{:S(2)}) copy-start(s32[16]{0:T(128)} %param.19) | copy-start | bytes 196
  7.2 19.2 %copy-start.5 = (s32[32]{0:T(128)S(1)}, s32[32]{0:T(128)}, u32[]{:S(2)}) copy-start(s32[32]{0:T(128)} %param.21) | copy-start | bytes 388
  7.2 152.9 %all-gather.4.cloned.1.call-start = ((), (), s32[]{:S(2)}) async-start(), calls=%async_computation.2 | async-start | bytes 7569408 | tf_op jit(solution)/shard_map/all_gather | solution.py:72
  8.0 234.8 %all-gather.8.cloned.1.call-start = ((), (), s32[]{:S(2)}) async-start(), calls=%async_computation.4 | async-start | bytes 3784704 | tf_op jit(solution)/shard_map/all_gather | solution.py:101
  8.7 336.3 %all-gather.6.cloned.1.call-start = ((), (), s32[]{:S(2)}) async-start(), calls=%async_computation.3 | async-start | bytes 7569408 | tf_op jit(solution)/shard_map/all_gather | solution.py:73
  13.0 108.2 %all-to-all-start = ((bf16[32,128,448]{1,2,0:T(8,128)(2,1)}), bf16[32,128,448]{1,2,0:T(8,128)(2,1)}, u32[]{:S(2)}, u32[]{:S(2)}) async-start(bf16[32,128,448]{1,2,0:T(8,128)(2,1)} %stack.2), calls=%async_computation | async-start | bytes 7340032 | tf_op jit(solution)/shard_map/all_to_all | solution.py:99
  25.6 432.0 %reduce-scatter.2.cloned.1.call-start = ((), (), s32[]{:S(2)}) async-start(), calls=%async_computation.5 | async-start | bytes 2064384 | tf_op jit(solution)/shard_map/reduce_scatter | solution.py:118
  28.2 105.9 %copy-start.8 = (bf16[256,448]{0,1:T(8,128)(2,1)S(1)}, bf16[256,448]{0,1:T(8,128)(2,1)}, u32[]{:S(2)}) copy-start(bf16[256,448]{0,1:T(8,128)(2,1)} %param.11) | copy-start | bytes 688132
  160.1 12.3 %copy-start.2 = (f32[2,256,4096]{2,1,0:T(8,128)S(1)}, f32[2,256,4096]{2,1,0:T(8,128)}, u32[]{:S(2)}) copy-start(f32[2,256,4096]{2,1,0:T(8,128)} %get-tuple-element.20) | copy-start | bytes 25165828
  160.1 12.3 %copy-start.3 = (pred[256,4096]{1,0:T(8,128)(4,1)S(1)}, pred[256,4096]{1,0:T(8,128)(4,1)}, u32[]{:S(2)}) copy-start(pred[256,4096]{1,0:T(8,128)(4,1)} %broadcast_compare_fusion) | copy-start | bytes 3145732
  172.3 2.7 copy-start.1
Sparse Core Ops, SparseCore 0:
  10.6 149.4 all-gather.3
  162.6 80.0 all-gather.7
  245.3 99.6 all-gather.5
  361.2 35.0 reduce-scatter.1
